TPU v7x, 32 devices: a whole 2x2x4 slice. The times are simulated.
32 devices in a mesh: clip: 2 (over y), patch: 4 (over z), head: 2 (over x), rep: 2 (over core).
Axes of the slice: x: 2, y: 2, z: 4, core: 2. Of those that a mesh axis runs over, the one named last changes fastest.
Arguments:
- tokens: bfloat16 [1024, 3072], P(('clip', 'patch', 'head', 'rep')), parts along dimension 0, may hold values from -24 to 24
- modulation: float32 [3, 3072], replicated, may hold values from -3 to 3
- in_weight: bfloat16 [3072, 16, 384], P(None, ('head', 'rep')), may hold values from -0.109375 to 0.109375
- query_gain: float32 [128], replicated, may hold values from 1 to 2.5
- key_gain: float32 [128], replicated, may hold values from 0.25 to 1.75
- out_weight: bfloat16 [16, 128, 3072], P(('head', 'rep')), may hold values from -1.5 to 1.5
- stale_cache: bfloat16 [1024, 16, 256], P(('clip', 'patch', 'head', 'rep')), parts along dimension 0, may hold values from -440 to 440, as said below
- lengths: int32 [8], P('clip'), parts along dimension 0, may hold values from 1 to 128, 384 in all
Outputs:
- update: bfloat16 [1024, 3072], P(('clip', 'patch', 'head', 'rep')), parts along dimension 0
- new_cache: bfloat16 [1024, 16, 256], P(('clip', 'patch', 'head', 'rep')), parts along dimension 0
There are 2 independent parts, one for each index of `clip`. A program takes and returns all parts, laid end to end along the dimension named above; an argument that names none is the same for every part. Nothing has to cross between parts.
Inputs may be any that keep to these rules, and one draw needn't show every extreme that they name: stale_cache[s, h] holds the stale key of token s and head h in its first 128 entries and the stale value in its last 128. Only the first lengths[p] tokens of patch p are live keys.
All inputs are finite; a program needn't handle non-finite values.
Results may differ from a plain program's by a relative error of at most 0.02.
The roundings to bfloat16 on the way count: a program that leaves them out, or rounds other values in their place, can miss the bound.
Values may be sent and summed in bfloat16 or wider, within the bound.
No kernel may reach another device: no remote copies, remote signals or barrier semaphores. Data moves between devices by JAX's collectives and lax.ppermute only.
A program may use at most 128 MiB of HBM per device.

v0:
```python
import math
import jax
import jax.numpy as jnp
from jax import lax
from jax.sharding import PartitionSpec as P

EPSILON = 1e-06
NEGATIVE = -1e30
key_block = 512


def normalize_rows(values):
    average = jnp.mean(values, axis=-1, keepdims=True)
    centred = values - average
    variance = jnp.mean(centred * centred, axis=-1, keepdims=True)
    return centred * lax.rsqrt(variance + EPSILON)


def rms_gain(values, gain):
    return values * lax.rsqrt(jnp.mean(values * values, axis=-1, keepdims=True) + EPSILON) * gain


def project(normed, in_weight, query_gain, key_gain):
    row_count = normed.shape[0]
    head_count = in_weight.shape[1]
    triple = in_weight.shape[2]
    head_dim = triple // 3
    flat_weight = in_weight.reshape(in_weight.shape[0], head_count * triple)
    projected = jnp.dot(normed, flat_weight, preferred_element_type=jnp.float32).reshape(
        row_count, head_count, triple
    )
    queries = rms_gain(projected[..., :head_dim], query_gain)
    fresh_keys = rms_gain(projected[..., head_dim : 2 * head_dim], key_gain)
    return jnp.concatenate([queries, fresh_keys, projected[..., 2 * head_dim :]], axis=-1).astype(
        jnp.bfloat16
    )


def lookup(lengths, patch_of):
    patch_ids = jnp.arange(lengths.shape[0], dtype=jnp.int32)
    return jnp.sum(jnp.where(patch_of[:, None] == patch_ids[None, :], lengths[None, :], 0), axis=1)


def attend(running, queries, key_rows, usable):
    head_dim = queries.shape[-1]
    row_max, denominator, weighted = running
    scores = jnp.einsum(
        "qhd,khd->qhk", queries, key_rows[..., :head_dim], preferred_element_type=jnp.float32
    )
    scores = scores * (1.0 / math.sqrt(head_dim))
    key_mask = usable[None, None, :]
    scores = jnp.where(key_mask, scores, NEGATIVE)
    new_max = jnp.maximum(row_max, jnp.max(scores, axis=-1))
    weights = jnp.where(key_mask, jnp.exp(scores - new_max[..., None]), 0.0)
    factor = jnp.exp(row_max - new_max)
    denominator = denominator * factor + jnp.sum(weights, axis=-1)
    weighted = weighted * factor[..., None] + jnp.einsum(
        "qhk,khd->qhd",
        weights.astype(jnp.bfloat16),
        key_rows[..., head_dim:],
        preferred_element_type=jnp.float32,
    )
    return (new_max, denominator, weighted)


def attend_blocks(running, queries, key_rows, usable):
    key_count = key_rows.shape[0]
    if key_count > key_block and key_count % key_block == 0:
        shaped = key_rows.reshape((key_count // key_block, key_block) + key_rows.shape[1:])
        usable_rows = usable.reshape(key_count // key_block, key_block)

        def step_block(current, operands):
            return (attend(current, queries, operands[0], operands[1]), None)

        running, _ = lax.scan(step_block, running, (shaped, usable_rows))
        return running
    return attend(running, queries, key_rows, usable)


def per_device(
    tokens, modulation, in_weight, query_gain, key_gain, out_weight, stale_cache, lengths
):
    heads_dev = in_weight.shape[1]
    head_dim = query_gain.shape[0]
    normed = (
        normalize_rows(tokens.astype(jnp.float32)) * (1.0 + modulation[1]) + modulation[0]
    ).astype(jnp.bfloat16)
    fresh = project(
        lax.all_gather(normed, ("head", "rep"), axis=0, tiled=True), in_weight, query_gain, key_gain
    )
    queries = fresh[..., :head_dim]
    own_rows = fresh[..., head_dim:]
    new_cache = lax.all_to_all(own_rows, ("head", "rep"), split_axis=0, concat_axis=1, tiled=True)
    patch_tok = fresh.shape[0]
    own_patch = lax.axis_index("patch")
    own_length = lookup(lengths, jnp.full((1,), own_patch, jnp.int32))[0]
    running = (
        jnp.full((patch_tok, heads_dev), NEGATIVE, jnp.float32),
        jnp.zeros((patch_tok, heads_dev), jnp.float32),
        jnp.zeros((patch_tok, heads_dev, head_dim), jnp.float32),
    )
    running = attend_blocks(
        running, queries, own_rows, jnp.arange(patch_tok, dtype=jnp.int32) < own_length
    )
    stale_heads = lax.all_to_all(
        stale_cache, ("head", "rep"), split_axis=1, concat_axis=0, tiled=True
    )
    shard_part = lax.all_gather(stale_heads, "patch", axis=0, tiled=True)
    key_index = jnp.arange(shard_part.shape[0], dtype=jnp.int32)
    patch_of = key_index // patch_tok
    position = key_index % patch_tok
    usable = (position < lookup(lengths, patch_of)) & (patch_of != own_patch)
    running = attend_blocks(running, queries, shard_part, usable)
    attended = (running[2] / running[1][..., None]).astype(jnp.bfloat16)
    flat_rows = attended.reshape(patch_tok, heads_dev * head_dim)
    flat_weight = out_weight.reshape(heads_dev * head_dim, out_weight.shape[2])
    attention = lax.psum_scatter(
        jnp.dot(flat_rows, flat_weight, preferred_element_type=jnp.float32).astype(jnp.bfloat16),
        ("head", "rep"),
        scatter_dimension=0,
        tiled=True,
    ).astype(jnp.float32)
    update = (modulation[2] * attention).astype(jnp.bfloat16)
    return (update, new_cache)


def solution(mesh):
    return jax.shard_map(
        per_device,
        mesh=mesh,
        in_specs=(
            P(("clip", "patch", "head", "rep"), None),
            P(),
            P(None, ("head", "rep"), None),
            P(),
            P(),
            P(("head", "rep"), None, None),
            P(("clip", "patch", "head", "rep"), None, None),
            P("clip"),
        ),
        out_specs=(
            P(("clip", "patch", "head", "rep"), None),
            P(("clip", "patch", "head", "rep"), None, None),
        ),
        check_vma=False,
    )
```

profile of v0, /device:TPU:0, one launch (start us, length us, event | category | flops | bytes accessed | tf_op | source)
XLA Modules:
  0.0 127.5 jit_solution(7977245236789460566)
XLA Ops:
  7.2 1.9 %copy.21 = bf16[32,16,256]{2,0,1:T(8,128)(2,1)} copy(bf16[32,16,256]{2,1,0:T(8,128)(2,1)} %param.14) | data formatting | bytes 524288 | tf_op args[6]
  9.1 4.2 %all-to-all-start = ((bf16[32,16,256]{2,0,1:T(8,128)(2,1)}), bf16[32,16,256]{2,0,1:T(8,128)(2,1)}, u32[]{:S(2)}, u32[]{:S(2)}) async-start(bf16[32,16,256]{2,0,1:T(8,128)(2,1)} %copy.21), calls=%async_computation | async-start | bytes 524288 | tf_op jit(solution)/shard_map/all_to_all | solution.py:105
  13.3 9.0 %copy.31 = bf16[384,8,4,384]{3,1,2,0:T(8,128)(2,1)} copy(bf16[384,8,4,384]{3,2,1,0:T(4,128)(2,1)} %bitcast.47) | data formatting | bytes 18874368
  22.3 12.7 %copy.18 = bf16[1536,3072]{1,0:T(8,128)(2,1)} copy(bf16[1536,3072]{0,1:T(8,128)(2,1)} %bitcast.46) | data formatting | bytes 18874368 | tf_op jit(solution)/shard_map/dot_general | solution.py:29
  35.6 9.9 %all_gather.6 = bf16[128,3072]{1,0:T(8,128)(2,1)S(1)} all-gather(bf16[32,3072]{1,0:T(8,128)(2,1)S(1)} %fusion.30), channel_id=1, replica_groups=mesh['clip'=2,'patch'=4,'head'=2,'rep'=2] {'head','rep'}, dimensions={0}, use_global_device_ids=true | all-gather | bytes 983040 | tf_op jit(solution)/shard_map/all_gather | solution.py:89
  45.6 7.8 %fusion.12 = f32[128,4,384]{2,0,1:T(8,128)} fusion(bf16[4,384,3072]{2,1,0:T(8,128)(2,1)} %bitcast.45, bf16[128,3072]{1,0:T(8,128)(2,1)S(1)} %all_gather.6), kind=kOutput, calls=%fused_computation.18 | convolution fusion | flops 1207959552 | bytes 11010048 | tf_op jit(solution)/shard_map/dot_general | solution.py:29
  54.0 1.7 %copy.22 = bf16[32,4,4,256]{3,0,1,2:T(8,128)(2,1)} copy(bf16[32,4,4,256]{3,0,2,1:T(8,128)(2,1)} %bitcast.8) | data formatting | bytes 524288 | tf_op jit(solution)/shard_map/all_to_all | solution.py:105
  55.7 0.7 iota_compare_fusion.1
  56.5 1.2 multiply_reduce_fusion
  58.4 1.1 multiply_convert_fusion.2
  59.5 1.8 %fusion.50 = (f32[128,4]{0,1:T(4,128)}, f32[128,4,128]{0,2,1:T(8,128)S(1)}) fusion(bf16[128,4,128]{2,0,1:T(8,128)(2,1)S(1)} %multiply_convert_fusion.2, f32[128,4,384]{2,0,1:T(8,128)} %fusion.12, f32[128]{0:T(128)} %param.11, f32[128,4]{0,1:T(4,128)S(1)} %add_rsqrt_fusion, pred[128]{0:T(512)(128)(4,1)S(1)} %iota_compare_fusion.1), kind=kOutput, calls=%fused_computation.77 | convolution fusion | flops 17169920 | bytes 660096 | tf_op jit(solution)/shard_map/qhd,khd->qhk/dot_general | solution.py:47
  61.3 24.1 %all-gather.2.cloned.1.call-done = bf16[512,4,256]{2,0,1:T(8,128)(2,1)} async-done(((bf16[128,4,256]{2,0,1:T(8,128)(2,1)}), bf16[512,4,256]{2,0,1:T(8,128)(2,1)}) %all-gather.2.cloned.1.call-update) | async-done | bytes 1048592 | tf_op jit(solution)/shard_map/all_gather | solution.py:108
  85.4 1.6 %fusion.51 = (f32[128,4]{0,1:T(4,128)S(1)}, f32[128,4,512]{2,0,1:T(8,128)S(1)}) fusion(bf16[512,4,256]{2,0,1:T(8,128)(2,1)} %all-gather.2.cloned.1.call-done, f32[128,4,384]{2,0,1:T(8,128)} %fusion.12, f32[128]{0:T(128)} %param.11, f32[128,4]{0,1:T(4,128)S(1)} %add_rsqrt_fusion, pred[512]{0:T(512)(128)(4,1)} %compare_and_fusion), kind=kOutput, calls=%fused_computation.78 | convolution fusion | flops 68091392 | bytes 1840128 | tf_op jit(solution)/shard_map/qhd,khd->qhk/dot_general | solution.py:47
  87.0 0.7 exponential_multiply_fusion
  88.0 1.0 fusion.10
  89.0 0.7 fusion.31
  89.7 1.3 %multiply_add_fusion = (f32[128,4]{0,1:T(4,128)}, f32[128,4]{0,1:T(4,128)S(1)}) fusion(f32[128,4]{0,1:T(4,128)S(1)} %fusion.10, f32[128,4]{0,1:T(4,128)S(1)} %fusion.31, f32[128,4]{0,1:T(4,128)} %get-tuple-element.12, f32[128,4]{0,1:T(4,128)S(1)} %get-tuple-element.14), kind=kLoop, calls=%fused_computation.56 | loop fusion | flops 4096 | bytes 12288 | tf_op jit(solution)/shard_map/add | solution.py:56
  91.0 1.9 %fusion.7 = f32[128,4,128]{0,2,1:T(8,128)} fusion(f32[128,4,128]{0,2,1:T(8,128)S(1)} %get-tuple-element.13, f32[128,4]{0,1:T(4,128)S(1)} %get-tuple-element.5, f32[128,4]{0,1:T(4,128)S(1)} %get-tuple-element.11, f32[128,4]{0,1:T(4,128)S(1)} %get-tuple-element.9, pred[128]{0:T(512)(128)(4,1)} %copy-done.4, f32[128,4,384]{2,0,1:T(8,128)} %fusion.12), kind=kOutput, calls=%fused_computation.12 | convolution fusion | flops 17104896 | bytes 662016 | tf_op jit(solution)/shard_map/qhk,khd->qhd/dot_general | solution.py:57
  92.9 3.3 %fusion = bf16[128,3072]{1,0:T(8,128)(2,1)} fusion(bf16[4,128,3072]{2,1,0:T(8,128)(2,1)S(1)} %copy-done, f32[128,4,128]{0,2,1:T(8,128)} %fusion.7, f32[128,4,512]{2,0,1:T(8,128)} %copy-done.1, bf16[512,4,256]{2,0,1:T(8,128)(2,1)} %all-gather.2.cloned.1.call-done, f32[128,4]{0,1:T(4,128)S(1)} %get-tuple-element.10, pred[512]{0:T(512)(128)(4,1)} %compare_and_fusion, ...), kind=kOutput, calls=%fused_computation.1 | convolution fusion | flops 471138304 | bytes 5771776 | tf_op jit(solution)/shard_map/dot_general | solution.py:118
  96.2 1.0 slice.68
  97.5 8.5 %all_to_all.36 = bf16[128,4,256]{2,1,0:T(4,128)(2,1)S(1)} all-to-all(bf16[128,4,256]{2,1,0:T(4,128)(2,1)S(1)} %copy.25), channel_id=1, replica_groups=mesh['clip'=2,'patch'=4,'head'=2,'rep'=2] {'head','rep'}, dimensions={0} | all-to-all | bytes 524288 | tf_op jit(solution)/shard_map/all_to_all | solution.py:93
  106.1 0.8 all_to_all.33
  106.9 12.1 %reduce-scatter.2.cloned.1.call-done = bf16[32,3072]{1,0:T(8,128)(2,1)} async-done(((bf16[128,3072]{1,0:T(8,128)(2,1)}), bf16[32,3072]{1,0:T(8,128)(2,1)}) %reduce-scatter.2.cloned.1.call-update) | async-done | bytes 196624 | tf_op jit(solution)/shard_map/reduce_scatter | solution.py:117
  119.0 1.6 %multiply_convert_fusion = bf16[32,3072]{1,0:T(8,128)(2,1)} fusion(bf16[32,3072]{1,0:T(8,128)(2,1)} %reduce-scatter.2.cloned.1.call-done, f32[3072]{0:T(1024)S(1)} %bitcast.50), kind=kLoop, calls=%fused_computation.33 | loop fusion | flops 294912 | bytes 405504 | tf_op jit(solution)/shard_map/convert_element_type | solution.py:123
  (34 shorter events, 2.6 us)
Async XLA Ops:
  7.2 85.8 %copy-start = (bf16[4,128,3072]{2,1,0:T(8,128)(2,1)S(1)}, bf16[4,128,3072]{2,1,0:T(8,128)(2,1)}, u32[]{:S(2)}) copy-start(bf16[4,128,3072]{2,1,0:T(8,128)(2,1)} %param.13) | copy-start | bytes 9437188
  9.1 44.9 %all-to-all-start = ((bf16[32,16,256]{2,0,1:T(8,128)(2,1)}), bf16[32,16,256]{2,0,1:T(8,128)(2,1)}, u32[]{:S(2)}, u32[]{:S(2)}) async-start(bf16[32,16,256]{2,0,1:T(8,128)(2,1)} %copy.21), calls=%async_computation | async-start | bytes 524288 | tf_op jit(solution)/shard_map/all_to_all | solution.py:105
  13.3 72.1 %all-gather.2.cloned.1.call-start = ((), (), s32[]{:S(2)}) async-start(), calls=%async_computation.3 | async-start | bytes 1310720 | tf_op jit(solution)/shard_map/all_gather | solution.py:108
  22.3 12.7 %copy-start.3 = (f32[3,3072]{1,0:T(4,128)S(1)}, f32[3,3072]{1,0:T(4,128)}, u32[]{:S(2)}) copy-start(f32[3,3072]{1,0:T(4,128)} %param.9) | copy-start | bytes 110596
  22.3 12.8 %copy-start.2 = (bf16[32,3072]{1,0:T(8,128)(2,1)S(1)}, bf16[32,3072]{1,0:T(8,128)(2,1)}, u32[]{:S(2)}) copy-start(bf16[32,3072]{1,0:T(8,128)(2,1)} %param.8) | copy-start | bytes 589828
  35.0 18.3 %copy-start.6 = (s32[4]{0:T(128)S(1)}, s32[4]{0:T(128)}, u32[]{:S(2)}) copy-start(s32[4]{0:T(128)} %param.15) | copy-start | bytes 52
  35.1 23.3 %copy-start.5 = (f32[128]{0:T(128)S(1)}, f32[128]{0:T(128)}, u32[]{:S(2)}) copy-start(f32[128]{0:T(128)} %param.12) | copy-start | bytes 1540
  55.7 63.3 %reduce-scatter.2.cloned.1.call-start = ((), (), s32[]{:S(2)}) async-start(), calls=%async_computation.4 | async-start | bytes 983040 | tf_op jit(solution)/shard_map/reduce_scatter | solution.py:117
  56.4 3.1 %copy-start.4 = (pred[128]{0:T(512)(128)(4,1)}, pred[128]{0:T(512)(128)(4,1)S(1)}, u32[]{:S(2)}) copy-start(pred[128]{0:T(512)(128)(4,1)S(1)} %iota_compare_fusion.1) | copy-start | bytes 388
  87.0 1.0 copy-start.1
Sparse Core Ops, SparseCore 0:
  55.8 29.5 all-gather.1
  96.4 22.5 reduce-scatter.1
where the time goes:
time: 128 us; the launch traced here: 127 us
  waiting for transfers between devices  36.3 us (28%)
  local copies, waits for them, and re-layouts  27.7 us (22%)
  blocking collectives  18.5 us (14%)
  matrix products  16.4 us (13%)
  between operations  14.2 us (11%)
  other arithmetic  10.2 us (8%)
  starting transfers between devices  4.28 us (3%)
    all_gather x1, waiting for transfers between devices, per_device(): shard_part = lax.all_gather(stale_heads, 'patch', axis=0, tiled=True)  24.1 us
    dot_general x1, local copies, waits for them, and re-layouts, project(): jnp.dot(normed, flat_weight, preferred_element_type=jnp.float32)  12.7 us
    reduce_scatter x1, waiting for transfers between devices, per_device(): lax.psum_scatter(jnp.dot(flat_rows, flat_weight, preferred_element_type=j...  12.1 us
    unnamed x16, local copies, waits for them, and re-layouts  11.2 us
    all_gather x1, blocking collectives, per_device(): lax.all_gather(normed, ('head', 'rep'), axis=0, tiled=True)  9.92 us
    all_to_all x1, blocking collectives, per_device(): lax.all_to_all(own_rows, ('head', 'rep'), split_axis=0, concat_axis=1, ti...  8.54 us
    dot_general x1, matrix products, project(): jnp.dot(normed, flat_weight, preferred_element_type=jnp.float32)  7.79 us
    all_to_all x1, starting transfers between devices, per_device(): lax.all_to_all(stale_cache, ('head', 'rep'), split_axis=1, concat_axis=0,...  4.24 us
  transfers between devices with their start and end apart: 3, of which 2 were waited for; matrix products, arithmetic and copies ran while one was open for 29% of the time, Pallas kernels for 0%

commit v1 on v0

--- a/solution.py
+++ b/solution.py
@@ -7,6 +7,17 @@
 EPSILON = 1e-06
 NEGATIVE = -1e30
 key_block = 512
+
+
+def gather_by_hops(x, axis, dim):
+    n_dev = lax.axis_size(axis)
+    hops = [(i, (i + 1) % n_dev) for i in range(n_dev)]
+    pieces = [x]
+    for far in range(1, n_dev):
+        pieces = [lax.ppermute(pieces[0], axis, hops), *pieces]
+    whole = jnp.concatenate(pieces, axis=dim)
+    shift = (lax.axis_index(axis) + 1) * pieces[-1].shape[dim]
+    return jnp.roll(whole, shift, axis=dim)
 
 
 def normalize_rows(values):
@@ -105,7 +116,7 @@
     stale_heads = lax.all_to_all(
         stale_cache, ("head", "rep"), split_axis=1, concat_axis=0, tiled=True
     )
-    shard_part = lax.all_gather(stale_heads, "patch", axis=0, tiled=True)
+    shard_part = gather_by_hops(stale_heads, "patch", 0)
     key_index = jnp.arange(shard_part.shape[0], dtype=jnp.int32)
     patch_of = key_index // patch_tok
     position = key_index % patch_tok

time: 128 us -> 127 us (level)
  local copies, waits for them, and re-layouts: 27.7 us -> 34.3 us
  matrix products: 16.4 us -> 12.2 us
  waiting for transfers between devices: 36.3 us -> 33 us
  other arithmetic: 10.2 us -> 7.44 us
  starting transfers between devices: 4.28 us -> 6.31 us
    all_gather x1 -> x0, waiting for transfers between devices: 24.1 us -> none  [per_device(): shard_part = lax.all_gather(stale_heads, 'patch', axis=0, tiled=True)]
    ppermute x0 -> x3, waiting for transfers between devices: none -> 22.5 us  [gather_by_hops(): pieces = [lax.ppermute(pieces[0], axis, hops), *pieces]]
    unnamed x16 -> x35, local copies, waits for them, and re-layouts: 11.2 us -> 18.6 us
    ppermute x0 -> x3, starting transfers between devices: none -> 2.07 us  [gather_by_hops(): pieces = [lax.ppermute(pieces[0], axis, hops), *pieces]]
    dot_general x2, matrix products: 3.42 us -> 1.71 us  [attend(): jnp.einsum('qhd,khd->qhk', queries, key_rows[..., :head_dim], preferred_e...]
    dot_general x1, matrix products: 1.92 us -> 0.27 us  [attend(): jnp.einsum('qhk,khd->qhd', weights.astype(jnp.bfloat16), key_rows[..., he...]
    reduce_scatter x1, waiting for transfers between devices: 12.1 us -> 10.5 us  [per_device(): lax.psum_scatter(jnp.dot(flat_rows, flat_weight, preferred_element_type=j...]
    reduce_sum x2, other arithmetic: 1.69 us -> 0.32 us  [attend(): denominator = denominator * factor + jnp.sum(weights, axis=-1)]
  transfers between devices with their start and end apart: 3 -> 5, of which waited for: 2 -> 4; matrix products, arithmetic and copies ran while one was open for 29% -> 29% of each run, Pallas kernels for 0% -> 0%
where the time goes in v1:
time: 127 us; the launch traced here: 126 us
  local copies, waits for them, and re-layouts  34.3 us (27%)
  waiting for transfers between devices  33 us (26%)
  blocking collectives  18.4 us (14%)
  between operations  14.3 us (11%)
  matrix products  12.2 us (10%)
  other arithmetic  7.44 us (6%)
  starting transfers between devices  6.31 us (5%)
    ppermute x3, waiting for transfers between devices, gather_by_hops(): pieces = [lax.ppermute(pieces[0], axis, hops), *pieces]  22.5 us
    unnamed x35, local copies, waits for them, and re-layouts  18.6 us
    dot_general x1, local copies, waits for them, and re-layouts, project(): jnp.dot(normed, flat_weight, preferred_element_type=jnp.float32)  12.7 us
    reduce_scatter x1, waiting for transfers between devices, per_device(): lax.psum_scatter(jnp.dot(flat_rows, flat_weight, preferred_element_type=j...  10.5 us
    all_gather x1, blocking collectives, per_device(): lax.all_gather(normed, ('head', 'rep'), axis=0, tiled=True)  9.93 us
    all_to_all x1, blocking collectives, per_device(): lax.all_to_all(own_rows, ('head', 'rep'), split_axis=0, concat_axis=1, ti...  8.43 us
    dot_general x1, matrix products, project(): jnp.dot(normed, flat_weight, preferred_element_type=jnp.float32)  6.91 us
    all_to_all x1, starting transfers between devices, per_device(): lax.all_to_all(stale_cache, ('head', 'rep'), split_axis=1, concat_axis=0,...  4.24 us
  transfers between devices with their start and end apart: 5, of which 4 were waited for; matrix products, arithmetic and copies ran while one was open for 29% of the time, Pallas kernels for 0%

profile of v1, /device:TPU:0, one launch (start us, length us, event | category | flops | bytes accessed | tf_op | source)
XLA Modules:
  0.0 125.9 jit_solution(1365148170852190958)
XLA Ops:
  7.2 1.9 %copy.21 = bf16[32,16,256]{2,0,1:T(8,128)(2,1)} copy(bf16[32,16,256]{2,1,0:T(8,128)(2,1)} %param.14) | data formatting | bytes 524288 | tf_op args[6]
  9.1 4.2 %all-to-all-start = ((bf16[32,16,256]{2,0,1:T(8,128)(2,1)}), bf16[32,16,256]{2,0,1:T(8,128)(2,1)}, u32[]{:S(2)}, u32[]{:S(2)}) async-start(bf16[32,16,256]{2,0,1:T(8,128)(2,1)} %copy.21), calls=%async_computation | async-start | bytes 524288 | tf_op jit(solution)/shard_map/all_to_all | solution.py:116
  13.3 9.0 %copy.33 = bf16[384,8,4,384]{3,1,2,0:T(8,128)(2,1)} copy(bf16[384,8,4,384]{3,2,1,0:T(4,128)(2,1)} %bitcast.47) | data formatting | bytes 18874368
  22.3 12.7 %copy.18 = bf16[1536,3072]{1,0:T(8,128)(2,1)} copy(bf16[1536,3072]{0,1:T(8,128)(2,1)} %bitcast.46) | data formatting | bytes 18874368 | tf_op jit(solution)/shard_map/dot_general | solution.py:40
  35.6 9.9 %all_gather.3 = bf16[128,3072]{1,0:T(8,128)(2,1)S(1)} all-gather(bf16[32,3072]{1,0:T(8,128)(2,1)S(1)} %fusion.30), channel_id=1, replica_groups=mesh['clip'=2,'patch'=4,'head'=2,'rep'=2] {'head','rep'}, dimensions={0}, use_global_device_ids=true | all-gather | bytes 983040 | tf_op jit(solution)/shard_map/all_gather | solution.py:100
  45.5 6.9 %fusion.12 = f32[128,4,384]{2,0,1:T(8,128)S(1)} fusion(bf16[4,384,3072]{2,1,0:T(8,128)(2,1)} %bitcast.45, bf16[128,3072]{1,0:T(8,128)(2,1)S(1)} %all_gather.3), kind=kOutput, calls=%fused_computation.18 | convolution fusion | flops 1207959552 | bytes 11010048 | tf_op jit(solution)/shard_map/dot_general | solution.py:40
  54.3 1.0 copy.22
  55.2 2.1 %collective-permute-start = (bf16[128,4,256]{2,0,1:T(8,128)(2,1)S(1)}, bf16[128,4,256]{2,0,1:T(8,128)(2,1)S(1)}, u32[]{:S(2)}, u32[]{:S(2)}) collective-permute-start(bf16[128,4,256]{2,0,1:T(8,128)(2,1)S(1)} %bitcast.48), channel_id=1, source_target_pairs={{0,4},{4,8},{8,12},{12,0},{1,5},{5,9},{9,13},{13,1},{2,6},{6,10},{... | collective-permute-start | bytes 786440 | tf_op jit(solution)/shard_map/ppermute | solution.py:17
  57.8 8.4 %collective-permute-done = bf16[128,4,256]{2,0,1:T(8,128)(2,1)S(1)} collective-permute-done((bf16[128,4,256]{2,0,1:T(8,128)(2,1)S(1)}, bf16[128,4,256]{2,0,1:T(8,128)(2,1)S(1)}, u32[]{:S(2)}, u32[]{:S(2)}) %collective-permute-start) | collective-permute-done | bytes 262176 | tf_op jit(solution)/shard_map/ppermute | solution.py:17
  67.5 1.1 multiply_convert_fusion.2
  68.6 7.4 %collective-permute-done.1 = bf16[128,4,256]{2,0,1:T(8,128)(2,1)} collective-permute-done((bf16[128,4,256]{2,0,1:T(8,128)(2,1)S(1)}, bf16[128,4,256]{2,0,1:T(8,128)(2,1)}, u32[]{:S(2)}, u32[]{:S(2)}) %collective-permute-start.1) | collective-permute-done | bytes 262176 | tf_op jit(solution)/shard_map/ppermute | solution.py:17
  76.0 1.1 iota_compare_fusion.1
  77.2 1.3 %fusion.53 = (f32[128,4]{0,1:T(4,128)S(1)}, f32[128,4,128]{0,2,1:T(8,128)S(1)}) fusion(bf16[128,4,128]{2,0,1:T(8,128)(2,1)S(1)} %multiply_convert_fusion.2, f32[128,4,384]{2,0,1:T(8,128)} %copy-done.2, f32[128]{0:T(128)} %param.11, f32[128,4]{0,1:T(4,128)S(1)} %add_rsqrt_fusion, pred[128]{0:T(512)(128)(4,1)} %iota_compare_fusion.1), kind=kOutput, calls=%fused_computation.87 | convolution fusion | flops 17169920 | bytes 660480 | tf_op jit(solution)/shard_map/qhd,khd->qhk/dot_general | solution.py:58
  78.5 6.8 %collective-permute-done.2 = bf16[128,4,256]{2,0,1:T(8,128)(2,1)} collective-permute-done((bf16[128,4,256]{2,0,1:T(8,128)(2,1)}, bf16[128,4,256]{2,0,1:T(8,128)(2,1)}, u32[]{:S(2)}, u32[]{:S(2)}) %collective-permute-start.2) | collective-permute-done | bytes 262176 | tf_op jit(solution)/shard_map/ppermute | solution.py:17
  86.3 1.0 constant_dynamic-update-slice_fusion.6
  87.2 1.0 constant_dynamic-update-slice_fusion.5
  88.2 1.0 constant_dynamic-update-slice_fusion.3
  89.2 1.0 constant_dynamic-update-slice_fusion.2
  90.7 1.2 copy-done.1
  93.2 3.3 %fusion = bf16[128,3072]{1,0:T(8,128)(2,1)} fusion(bf16[4,128,3072]{2,1,0:T(8,128)(2,1)S(1)} %copy-done, f32[128,4,128]{0,2,1:T(8,128)S(1)} %fusion.7, f32[128,4,512]{0,2,1:T(8,128)} %copy-done.1, bf16[1024,4,256]{2,0,1:T(8,128)(2,1)} %copy-done.7, s32[]{:T(128)S(6)} %select_n.75, s32[]{:T(128)S(6)} %add.115, f32[128,4]{0,1:T(4,128)S(1)} %get-tuple-element.10, ...), kind=kOutput, calls=%fused_computation.1 | convolution fusion | flops 471138304 | bytes 5771784 | tf_op jit(solution)/shard_map/dot_general | solution.py:129
  96.5 1.0 slice.61
  97.7 8.4 %all_to_all.36 = bf16[128,4,256]{2,1,0:T(4,128)(2,1)S(1)} all-to-all(bf16[128,4,256]{2,1,0:T(4,128)(2,1)S(1)} %copy.26), channel_id=1, replica_groups=mesh['clip'=2,'patch'=4,'head'=2,'rep'=2] {'head','rep'}, dimensions={0} | all-to-all | bytes 524288 | tf_op jit(solution)/shard_map/all_to_all | solution.py:104
  107.0 10.5 %reduce-scatter.2.cloned.1.call-done = bf16[32,3072]{1,0:T(8,128)(2,1)} async-done(((bf16[128,3072]{1,0:T(8,128)(2,1)}), bf16[32,3072]{1,0:T(8,128)(2,1)}) %reduce-scatter.2.cloned.1.call-update) | async-done | bytes 196624 | tf_op jit(solution)/shard_map/reduce_scatter | solution.py:128
  117.5 1.6 %multiply_convert_fusion = bf16[32,3072]{1,0:T(8,128)(2,1)} fusion(bf16[32,3072]{1,0:T(8,128)(2,1)} %reduce-scatter.2.cloned.1.call-done, f32[3072]{0:T(1024)S(1)} %bitcast.52), kind=kLoop, calls=%fused_computation.33 | loop fusion | flops 294912 | bytes 405504 | tf_op jit(solution)/shard_map/convert_element_type | solution.py:134
  (57 shorter events, 8.0 us)
Async XLA Ops:
  7.2 86.0 %copy-start = (bf16[4,128,3072]{2,1,0:T(8,128)(2,1)S(1)}, bf16[4,128,3072]{2,1,0:T(8,128)(2,1)}, u32[]{:S(2)}) copy-start(bf16[4,128,3072]{2,1,0:T(8,128)(2,1)} %param.13) | copy-start | bytes 9437188
  9.1 45.2 %all-to-all-start = ((bf16[32,16,256]{2,0,1:T(8,128)(2,1)}), bf16[32,16,256]{2,0,1:T(8,128)(2,1)}, u32[]{:S(2)}, u32[]{:S(2)}) async-start(bf16[32,16,256]{2,0,1:T(8,128)(2,1)} %copy.21), calls=%async_computation | async-start | bytes 524288 | tf_op jit(solution)/shard_map/all_to_all | solution.py:116
  13.3 104.2 %reduce-scatter.2.cloned.1.call-start = ((), (), s32[]{:S(2)}) async-start(), calls=%async_computation.3 | async-start | bytes 983040 | tf_op jit(solution)/shard_map/reduce_scatter | solution.py:128
  22.3 12.8 %copy-start.8 = (f32[3,3072]{1,0:T(4,128)S(1)}, f32[3,3072]{1,0:T(4,128)}, u32[]{:S(2)}) copy-start(f32[3,3072]{1,0:T(4,128)} %param.9) | copy-start | bytes 110596
  22.3 12.8 %copy-start.4 = (bf16[32,3072]{1,0:T(8,128)(2,1)S(1)}, bf16[32,3072]{1,0:T(8,128)(2,1)}, u32[]{:S(2)}) copy-start(bf16[32,3072]{1,0:T(8,128)(2,1)} %param.8) | copy-start | bytes 589828
  45.5 8.0 %copy-start.12 = (s32[4]{0:T(128)S(1)}, s32[4]{0:T(128)}, u32[]{:S(2)}) copy-start(s32[4]{0:T(128)} %param.15) | copy-start | bytes 52
  52.5 0.9 copy-start.2
  55.2 10.9 %collective-permute-start = (bf16[128,4,256]{2,0,1:T(8,128)(2,1)S(1)}, bf16[128,4,256]{2,0,1:T(8,128)(2,1)S(1)}, u32[]{:S(2)}, u32[]{:S(2)}) collective-permute-start(bf16[128,4,256]{2,0,1:T(8,128)(2,1)S(1)} %bitcast.48), channel_id=1, source_target_pairs={{0,4},{4,8},{8,12},{12,0},{1,5},{5,9},{9,13},{13,1},{2,6},{6,10},{... | collective-permute-start | bytes 786440 | tf_op jit(solution)/shard_map/ppermute | solution.py:17
  66.1 0.7 copy-start.5
  66.2 9.9 %collective-permute-start.1 = (bf16[128,4,256]{2,0,1:T(8,128)(2,1)S(1)}, bf16[128,4,256]{2,0,1:T(8,128)(2,1)}, u32[]{:S(2)}, u32[]{:S(2)}) collective-permute-start(bf16[128,4,256]{2,0,1:T(8,128)(2,1)S(1)} %collective-permute-done), channel_id=1, source_target_pairs={{0,4},{4,8},{8,12},{12,0},{1,5},{5,9},{9,13},{13,1},{2,6},{6,10},{... | collective-permute-start | bytes 786440 | tf_op jit(solution)/shard_map/ppermute | solution.py:17
  76.0 9.2 %collective-permute-start.2 = (bf16[128,4,256]{2,0,1:T(8,128)(2,1)}, bf16[128,4,256]{2,0,1:T(8,128)(2,1)}, u32[]{:S(2)}, u32[]{:S(2)}) collective-permute-start(bf16[128,4,256]{2,0,1:T(8,128)(2,1)} %collective-permute-done.1), channel_id=1, source_target_pairs={{0,4},{4,8},{8,12},{12,0},{1,5},{5,9},{9,13},{13,1},{2,6},{6,10},{... | collective-permute-start | bytes 786440 | tf_op jit(solution)/shard_map/ppermute | solution.py:17
  77.2 13.0 %copy-start.6 = (bf16[128,4,256]{2,0,1:T(8,128)(2,1)S(1)}, bf16[128,4,256]{2,0,1:T(8,128)(2,1)}, u32[]{:S(2)}) copy-start(bf16[128,4,256]{2,0,1:T(8,128)(2,1)} %copy-done.5) | copy-start | bytes 786436
  78.5 11.8 %copy-start.3 = (f32[128,4,384]{2,0,1:T(8,128)S(1)}, f32[128,4,384]{2,0,1:T(8,128)}, u32[]{:S(2)}) copy-start(f32[128,4,384]{2,0,1:T(8,128)} %copy-done.2) | copy-start | bytes 2359300
  78.5 11.8 %copy-start.9 = (pred[512]{0:T(512)(128)(4,1)S(1)}, pred[512]{0:T(512)(128)(4,1)}, u32[]{:S(2)}) copy-start(pred[512]{0:T(512)(128)(4,1)} %compare_and_fusion) | copy-start | bytes 1540
  78.5 11.8 %copy-start.11 = (f32[128]{0:T(128)S(1)}, f32[128]{0:T(128)}, u32[]{:S(2)}) copy-start(f32[128]{0:T(128)} %param.11) | copy-start | bytes 1540
  90.2 2.0 %copy-start.10 = (pred[128]{0:T(512)(128)(4,1)S(1)}, pred[128]{0:T(512)(128)(4,1)}, u32[]{:S(2)}) copy-start(pred[128]{0:T(512)(128)(4,1)} %iota_compare_fusion.1) | copy-start | bytes 388
  90.3 2.9 %copy-start.7 = (bf16[1024,4,256]{2,0,1:T(8,128)(2,1)}, bf16[1024,4,256]{2,0,1:T(8,128)(2,1)S(1)}, u32[]{:S(2)}) copy-start(bf16[1024,4,256]{2,0,1:T(8,128)(2,1)S(1)} %constant_dynamic-update-slice_fusion) | copy-start | bytes 6291460
  90.7 1.2 copy-start.1
Sparse Core Ops, SparseCore 0:
  96.6 20.8 reduce-scatter.1
